TPU v7x, 32 devices: a whole 2x2x4 slice. The times are simulated.
32 devices in a mesh: shard: 8 (over y, x, core), rep: 4 (over z).
Axes of the slice: x: 2, y: 2, z: 4, core: 2. Of those that a mesh axis runs over, the one named last changes fastest.
Arguments:
- tokens: bfloat16 [4, 1024, 1600], P('rep', 'shard'), may hold values from -6 to 6
- segment_ids: int32 [4, 1024], P('rep'), may hold values from 0 to 3, never falling along the last dimension, each value on 1 to 512 neighbouring positions
- ln1_gain: bfloat16 [1600], P('shard'), may hold values from 0.5 to 1.5
- ln1_bias: bfloat16 [1600], P('shard'), may hold values from -2.5 to 2.5
- w_qkv: bfloat16 [1600, 4800], P('shard')
- q_bias: bfloat16 [1600], P('shard'), may hold values from -2.5 to 2.5
- v_bias: bfloat16 [1600], P('shard'), may hold values from -2.5 to 2.5
- w_out: bfloat16 [1600, 1600], P('shard'), may hold values from -0.625 to 0.625
- out_bias: bfloat16 [1600], P('shard'), may hold values from -2.5 to 2.5
- ln2_gain: bfloat16 [1600], P('shard'), may hold values from 0.5 to 1.5
- ln2_bias: bfloat16 [1600], P('shard'), may hold values from -2.5 to 2.5
- w_fc: bfloat16 [1600, 6400], P('shard'), may hold values from -0.15625 to 0.15625
- fc_bias: bfloat16 [6400], P('shard'), may hold values from -2.5 to 2.5
- w_proj: bfloat16 [6400, 1600], P('shard'), may hold values from -0.078125 to 0.078125
- proj_bias: bfloat16 [1600], P('shard'), may hold values from -2.5 to 2.5
- grad_out: bfloat16 [4, 1024, 1600], P('rep', 'shard'), may hold values from -6 to 6
Outputs:
- output: float32 [4, 1024, 1600], P('rep', 'shard')
- grad_tokens: float32 [4, 1024, 1600], P('rep', 'shard')
- grad_ln1_gain: float32 [1600], P('shard')
- grad_ln1_bias: float32 [1600], P('shard')
- grad_w_qkv: float32 [1600, 4800], P('shard', 'rep')
- grad_q_bias: float32 [1600], P('shard')
- grad_v_bias: float32 [1600], P('shard')
- grad_w_out: float32 [1600, 1600], P('shard', 'rep')
- grad_out_bias: float32 [1600], P('shard')
- grad_ln2_gain: float32 [1600], P('shard')
- grad_ln2_bias: float32 [1600], P('shard')
- grad_w_fc: float32 [1600, 6400], P('shard', 'rep')
- grad_fc_bias: float32 [6400], P('shard')
- grad_w_proj: float32 [6400, 1600], P('shard', 'rep')
- grad_proj_bias: float32 [1600], P('shard')
Inputs may be any that keep to these rules, and one draw needn't show every extreme that they name: `segment_ids`: along each sequence the document numbers never fall, and one document covers at most 512 positions.
All inputs are finite; a program needn't handle non-finite values.
Results may differ from a plain program's by a relative error of at most 0.019.
Values may be sent and summed in bfloat16 or wider, within the bound.
No kernel may reach another device: no remote copies, remote signals or barrier semaphores. Data moves between devices by JAX's collectives and lax.ppermute only.
A program may use at most 576 MiB of HBM per device.

v0:
```python
import functools
import math

import jax
import jax.numpy as jnp
from jax import lax
from jax.experimental import pallas as pl
from jax.experimental.pallas import tpu as pltpu
from jax.sharding import PartitionSpec as P


HD = 64
MAX_DOC = 512

EPSILON = 1e-05
GELU_SCALE = math.sqrt(2.0 / math.pi)
BF16 = jnp.bfloat16
F32 = jnp.float32
NEG = -1e30
PAIR = 2 * HD


def layer_norm(values, gain, shift):
    centre_val = jnp.mean(values, axis=-1, keepdims=True)
    centred = values - centre_val
    variance = jnp.mean(centred * centred, axis=-1, keepdims=True)
    inverse = lax.rsqrt(variance + EPSILON)
    normed = centred * inverse
    return (normed * gain + shift, normed, inverse)


def norm_back(upstream, normed, inverse, gain):
    scaled = upstream * gain
    return inverse * (
        scaled
        - jnp.mean(scaled, axis=-1, keepdims=True)
        - normed * jnp.mean(scaled * normed, axis=-1, keepdims=True)
    )


def gelu_both(inputs_pre):
    square = inputs_pre * inputs_pre
    tangent = jnp.tanh(GELU_SCALE * (inputs_pre + 0.044715 * square * inputs_pre))
    value = 0.5 * inputs_pre * (1.0 + tangent)
    slope = 0.5 * (1.0 + tangent) + 0.5 * inputs_pre * (1.0 - tangent * tangent) * GELU_SCALE * (
        1.0 + 3.0 * 0.044715 * square
    )
    return value, slope


def dot_nn(a, b):
    return lax.dot_general(a, b, (((1,), (0,)), ((), ())), preferred_element_type=F32)


def dot_nt(a, b):
    return lax.dot_general(a, b, (((1,), (1,)), ((), ())), preferred_element_type=F32)


def dot_tn(a, b):
    return lax.dot_general(a, b, (((0,), (0,)), ((), ())), preferred_element_type=F32)


def block_at(me, j, count):
    k = jnp.bitwise_xor(me, j)
    return jnp.bitwise_and(k, 1) * (count // 2) + jnp.right_shift(k, 1)


def window_of(i, rows):
    back = -(-MAX_DOC // rows)
    return max(0, i - back) * rows, (i + 1) * rows


def mask_of(seg_row, seg_col, i, rows):
    lo, hi = window_of(i, rows)
    first = i * rows
    query_pos = first + lax.broadcasted_iota(jnp.int32, (rows, hi - lo), 0)
    key_pos = lo + lax.broadcasted_iota(jnp.int32, (rows, hi - lo), 1)
    same = seg_col[first : first + rows, :] == seg_row[:, lo:hi]
    return (key_pos <= query_pos) & same


def fwd_kernel(scale, rows, me_ref, seg_row, seg_col, qkv_ref, out_ref, lse_ref, ks, vs):
    count, part, width = qkv_ref.shape
    third = width // 3
    me = me_ref[0]
    spots = [block_at(me, j, count) for j in range(count)]
    per = rows // part
    left = lax.broadcasted_iota(jnp.int32, (1, PAIR), 1) < HD
    for pair in range(third // PAIR):
        at = pair * PAIR
        for j in range(count):
            ks[j * part : (j + 1) * part, :] = qkv_ref[spots[j], :, third + at : third + at + PAIR]
            vs[j * part : (j + 1) * part, :] = qkv_ref[
                spots[j], :, 2 * third + at : 2 * third + at + PAIR
            ]
        for i in range(count // per):
            lo, hi = window_of(i, rows)
            mask = mask_of(seg_row, seg_col, i, rows)
            q = jnp.concatenate(
                [qkv_ref[spots[i * per + b], :, at : at + PAIR] for b in range(per)], axis=0
            )
            kk, vv = ks[lo:hi, :], vs[lo:hi, :]
            mixed, totals = [], []
            for side in (left, ~left):
                qm = jnp.where(side, q, jnp.zeros_like(q))
                s = jnp.where(mask, dot_nt(qm, kk) * scale, NEG)
                top = jnp.max(s, axis=-1, keepdims=True)
                e = jnp.exp(s - top)
                total = jnp.sum(e, axis=-1, keepdims=True)
                mixed.append(dot_nn((e * (1.0 / total)).astype(BF16), vv))
                totals.append(top + jnp.log(total))
            o = jnp.where(left, mixed[0], mixed[1]).astype(BF16)
            t = jnp.where(left, totals[0], totals[1])
            for b in range(per):
                out_ref[spots[i * per + b], :, at : at + PAIR] = o[b * part : (b + 1) * part, :]
                lse_ref[spots[i * per + b], :, at : at + PAIR] = t[b * part : (b + 1) * part, :]


def bwd_kernel(
    scale, rows, me_ref, seg_row, seg_col, qkv_ref, grad_ref, lse_ref, out_ref, sum_ref, ks, vs, dk, dv
):
    count, part, width = qkv_ref.shape
    third = width // 3
    me = me_ref[0]
    spots = [block_at(me, j, count) for j in range(count)]
    per = rows // part
    left = lax.broadcasted_iota(jnp.int32, (1, PAIR), 1) < HD
    sum_ref[...] = jnp.zeros_like(sum_ref)
    for pair in range(third // PAIR):
        at = pair * PAIR
        for j in range(count):
            ks[j * part : (j + 1) * part, :] = qkv_ref[spots[j], :, third + at : third + at + PAIR]
            vs[j * part : (j + 1) * part, :] = qkv_ref[
                spots[j], :, 2 * third + at : 2 * third + at + PAIR
            ]
        dk[...] = jnp.zeros_like(dk)
        dv[...] = jnp.zeros_like(dv)
        q_sum = jnp.zeros((1, PAIR), F32)
        for i in range(count // per):
            lo, hi = window_of(i, rows)
            mask = mask_of(seg_row, seg_col, i, rows)
            here = [spots[i * per + b] for b in range(per)]
            q = jnp.concatenate([qkv_ref[h, :, at : at + PAIR] for h in here], axis=0)
            g = jnp.concatenate([grad_ref[h, :, at : at + PAIR] for h in here], axis=0)
            t = jnp.concatenate([lse_ref[h, :, at : at + PAIR] for h in here], axis=0)
            kk, vv = ks[lo:hi, :], vs[lo:hi, :]
            dq = None
            for number, side in enumerate((left, ~left)):
                qm = jnp.where(side, q, jnp.zeros_like(q))
                gm = jnp.where(side, g, jnp.zeros_like(g))
                km = jnp.where(side, kk, jnp.zeros_like(kk))
                lse = t[:, number * HD : number * HD + 1]
                probs = jnp.where(mask, jnp.exp(dot_nt(qm, kk) * scale - lse), 0.0)
                dp = dot_nt(gm, vv)
                delta = jnp.sum(probs * dp, axis=-1, keepdims=True)
                ds = (probs * (dp - delta) * scale).astype(BF16)
                part_q = dot_nn(ds, km)
                dq = part_q if dq is None else dq + part_q
                dk[lo:hi, :] += dot_tn(ds, qm)
                dv[lo:hi, :] += dot_tn(probs.astype(BF16), gm)
            q_sum = q_sum + jnp.sum(dq, axis=0, keepdims=True)
            dq = dq.astype(BF16)
            for b in range(per):
                out_ref[here[b], :, at : at + PAIR] = dq[b * part : (b + 1) * part, :]
        sum_ref[0:1, at : at + PAIR] = q_sum
        sum_ref[0:1, third + at : third + at + PAIR] = jnp.sum(dk[...], axis=0, keepdims=True)
        sum_ref[0:1, 2 * third + at : 2 * third + at + PAIR] = jnp.sum(
            dv[...], axis=0, keepdims=True
        )
        for j in range(count):
            out_ref[spots[j], :, third + at : third + at + PAIR] = dk[
                j * part : (j + 1) * part, :
            ].astype(BF16)
            out_ref[spots[j], :, 2 * third + at : 2 * third + at + PAIR] = dv[
                j * part : (j + 1) * part, :
            ].astype(BF16)


def attention_calls(count, part, slots, scale):
    length = count * part
    rows = 2 * part
    third = slots * HD
    vm = pl.BlockSpec(memory_space=pltpu.VMEM)
    sm = pl.BlockSpec(memory_space=pltpu.SMEM)
    fwd = pl.pallas_call(
        functools.partial(fwd_kernel, scale, rows),
        out_shape=(
            jax.ShapeDtypeStruct((count, part, third), BF16),
            jax.ShapeDtypeStruct((count, part, third), F32),
        ),
        in_specs=[sm, vm, vm, vm],
        out_specs=(vm, vm),
        scratch_shapes=[pltpu.VMEM((length, PAIR), BF16)] * 2,
        cost_estimate=pl.CostEstimate(
            flops=4 * length * length * third,
            bytes_accessed=length * third * 14,
            transcendentals=length * length * slots,
        ),
    )
    bwd = pl.pallas_call(
        functools.partial(bwd_kernel, scale, rows),
        out_shape=(
            jax.ShapeDtypeStruct((count, part, 3 * third), BF16),
            jax.ShapeDtypeStruct((8, 3 * third), F32),
        ),
        in_specs=[sm, vm, vm, vm, vm, vm],
        out_specs=(vm, vm),
        scratch_shapes=[pltpu.VMEM((length, PAIR), BF16)] * 2
        + [pltpu.VMEM((length, PAIR), F32)] * 2,
        cost_estimate=pl.CostEstimate(
            flops=10 * length * length * third,
            bytes_accessed=length * third * 18,
            transcendentals=length * length * slots,
        ),
    )
    return fwd, bwd


def pack_kernel(cuts, halves, base_ref, src_ref, out_ref):
    count, rows, width = out_ref.shape
    for d, runs in enumerate(cuts):
        place = jnp.bitwise_xor(base_ref[0], d)
        if halves:
            place = halves_order(place, len(cuts))

        @pl.when(place < count)
        def _(runs=runs, place=place):
            if sum(hi - lo for lo, hi, _ in runs) < width:
                out_ref[place] = jnp.zeros((rows, width), out_ref.dtype)
            for lo, hi, at in runs:
                out_ref[place, :, at : at + hi - lo] = src_ref[:, lo:hi]


def pack(src, base, halves, cuts, count, width):
    rows = src.shape[0]
    return pl.pallas_call(
        functools.partial(pack_kernel, cuts, halves),
        out_shape=jax.ShapeDtypeStruct((count, rows, width), src.dtype),
        in_specs=[pl.BlockSpec(memory_space=pltpu.SMEM), pl.BlockSpec(memory_space=pltpu.VMEM)],
        out_specs=pl.BlockSpec(memory_space=pltpu.VMEM),
        cost_estimate=pl.CostEstimate(
            flops=0, bytes_accessed=2 * src.size + 2 * count * rows * width, transcendentals=0
        ),
    )(base.astype(jnp.int32).reshape(1), src)


def share_kernel(plan, extra_at, share, room, me_ref, *refs):
    *sources, local_ref, tail_ref, out_ref, src_ref = refs
    place_blocks(me_ref[0], sources, src_ref)
    tail = out_ref.shape[2] - share - room
    extra = src_ref[0, :, extra_at:].astype(F32)
    for k in range(1, src_ref.shape[0]):
        extra = extra + src_ref[k, :, extra_at:].astype(F32)
    extra = (extra + local_ref[...]).astype(BF16)
    for q, runs in enumerate(plan):
        for d, lo, hi, at in runs:
            out_ref[q, :, at : at + hi - lo] = src_ref[d, :, lo:hi]
        out_ref[q, :, share : share + room] = extra[:, :room]
        out_ref[q, :, share + room :] = tail_ref[:, q * tail : (q + 1) * tail]


def to_shares(sources, me_word, local, tail, plan, extra_at, share, room):
    n = lax.axis_size("shard")
    rows, width = sources[0].shape[1:]
    each = share + room + tail.shape[1] // len(plan)
    vm = pl.BlockSpec(memory_space=pltpu.VMEM)
    return pl.pallas_call(
        functools.partial(share_kernel, plan, extra_at, share, room),
        out_shape=jax.ShapeDtypeStruct((len(plan), rows, each), BF16),
        in_specs=[pl.BlockSpec(memory_space=pltpu.SMEM), *source_specs(sources), vm, vm],
        out_specs=vm,
        scratch_shapes=[pltpu.VMEM((n, rows, width), BF16)],
        cost_estimate=pl.CostEstimate(
            flops=0, bytes_accessed=4 * n * rows * width, transcendentals=0
        ),
    )(me_word, *sources, local, tail)


def exchange(x, k):
    n = lax.axis_size("shard")
    return lax.ppermute(x, "shard", [(i, i ^ k) for i in range(n)])


def gather_halves(x):
    n = lax.axis_size("shard")
    others = [exchange(x, k) for k in range(2, n, 2)]
    near = jnp.concatenate([x] + others, axis=0)
    return near, exchange(near, 1)


def chip_sums(far, near):
    return near + exchange(far, 1).astype(F32)


def finish_sums(total, hold=None):
    n = lax.axis_size("shard")
    rows = total.shape[0] // (n // 2)
    out = total[:rows]
    for i, k in enumerate(range(2, n, 2)):
        send = total[(i + 1) * rows : (i + 2) * rows].astype(BF16)
        if hold is not None:
            send = after(send, hold)
        out = out + exchange(send, k).astype(F32)
    return out


def halves_order(k, n):
    return jnp.bitwise_and(k, 1) * (n // 2) + jnp.right_shift(k, 1)


def swap_packed(packed):
    n = lax.axis_size("shard")
    near = packed[: n // 2]
    got = exchange(packed[n // 2 :], 1)
    pairs = [
        exchange(jnp.stack([near[i], got[i]]), 2 * i) for i in range(1, n // 2)
    ]
    return (packed[:1], got[:1], *pairs)


def place_blocks(me, sources, dest_ref):
    for i, source in enumerate(sources):
        for k in range(1 if i < 2 else 2):
            there = jnp.bitwise_xor(me, i if i < 2 else 2 * i - 2 + k)
            dest_ref[there] = source[k]


def source_specs(sources):
    return [pl.BlockSpec(memory_space=pltpu.VMEM)] * len(sources)


def unpack_kernel(me_ref, *refs):
    place_blocks(me_ref[0], refs[:-1], refs[-1])


def unpack(sources):
    n = lax.axis_size("shard")
    shape = (n, *sources[0].shape[1:])
    size = math.prod(shape)
    return pl.pallas_call(
        unpack_kernel,
        out_shape=jax.ShapeDtypeStruct(shape, BF16),
        in_specs=[pl.BlockSpec(memory_space=pltpu.SMEM), *source_specs(sources)],
        out_specs=pl.BlockSpec(memory_space=pltpu.VMEM),
        cost_estimate=pl.CostEstimate(flops=0, bytes_accessed=4 * size, transcendentals=0),
    )(lax.axis_index("shard").astype(jnp.int32).reshape(1), *sources)


def pick(blocks, i):
    return lax.dynamic_index_in_dim(blocks, i, 0, keepdims=False)


def rep_scatter(blocks):
    return lax.psum_scatter(blocks, "rep", scatter_dimension=0).astype(F32)


def jointly(x, where):
    n, n_rep = lax.axis_size("shard"), lax.axis_size("rep")
    pairs = []
    for s in range(n):
        for r in range(n_rep):
            to_s, to_r = where(s, r)
            pairs.append((s * n_rep + r, to_s * n_rep + to_r))
    return lax.ppermute(x, ("shard", "rep"), pairs)


def by_parity(pair):
    even = jnp.bitwise_and(lax.axis_index("shard"), 1) == 0
    return jnp.where(even, pair[0], pair[1]), jnp.where(even, pair[1], pair[0])


def spread_columns(rows, own):
    n, n_rep = lax.axis_size("shard"), lax.axis_size("rep")
    cuts = [[(d * own, (d + 1) * own, 0)] for d in range(n)]
    if n != 2 * n_rep:
        packed = pack(rows, lax.axis_index("shard"), True, cuts, n, own)
        return unpack(swap_packed(packed)).reshape(-1, own)
    s, r = lax.axis_index("shard"), lax.axis_index("rep")
    mine = pack(rows, jnp.bitwise_xor(s, 2 * r), False, cuts, 2, own)
    pair = [
        jointly(mine[k], lambda i, j, k=k: (i ^ (2 * j + k), j)) for k in range(2)
    ]
    mine = jnp.stack(by_parity(pair))
    chip = jnp.right_shift(s, 1)
    everyone = lax.all_gather(mine, "rep", axis=0)
    return jnp.concatenate(
        [pick(everyone, jnp.bitwise_xor(chip, c)) for c in range(n_rep)], axis=0
    ).reshape(-1, own)


def to_halves(blocks):
    n = blocks.shape[0]
    me = lax.axis_index("shard")
    order = [*range(0, n, 2), *range(1, n, 2)]
    return jnp.stack([pick(blocks, jnp.bitwise_xor(me, k)) for k in order])


def collect_rows(part, own_rows, total_columns, hold=None):
    n, n_rep = lax.axis_size("shard"), lax.axis_size("rep")
    own = part.shape[1]
    if n == 2 * n_rep:
        summed = rep_scatter(part.reshape(n_rep, 2, own_rows, own)).astype(BF16)
        if hold is not None:
            summed = after(summed, hold)
        even = jnp.bitwise_and(lax.axis_index("shard"), 1) == 0
        pair = []
        for k in range(2):
            sent = jnp.where(even, summed[k], summed[1 - k])
            pair.append(jointly(sent, lambda i, j, k=k: (2 * j + ((i & 1) ^ k), i >> 1)))
        return jnp.concatenate(by_parity(pair), axis=1).astype(F32)
    swapped = unpack(swap_packed(to_halves(part.reshape(n, own_rows, own))))
    if n_rep <= n:
        swapped = swapped.reshape(n_rep, n // n_rep, own_rows, own)
        total = rep_scatter(swapped)
        return total.transpose(1, 0, 2).reshape(own_rows, total_columns // n_rep)
    swapped = swapped.reshape(n, own_rows, n_rep // n, total_columns // n_rep)
    return rep_scatter(swapped.transpose(0, 2, 1, 3).reshape(n_rep, own_rows, -1))


def after(value, *others):
    return lax.optimization_barrier((value,) + others)[0]


def local(
    tokens,
    segment_ids,
    ln1_gain,
    ln1_bias,
    w_qkv,
    q_bias,
    v_bias,
    w_out,
    out_bias,
    ln2_gain,
    ln2_bias,
    w_fc,
    fc_bias,
    w_proj,
    proj_bias,
    grad_out,
):
    seq_count, part, width = tokens.shape
    length = segment_ids.shape[1]
    n = lax.axis_size("shard")
    n_rep = lax.axis_size("rep")
    me = lax.axis_index("shard")
    own = ln1_gain.shape[0]
    own_hidden = fc_bias.shape[0]
    hidden_width = w_fc.shape[1]
    scale = float(HD) ** (-0.5)

    first_head = [-(-own * d // HD) for d in range(n + 1)]
    n_heads = [first_head[d + 1] - first_head[d] for d in range(n)]
    slots = 2 * -(-max(n_heads) // 2)
    third = slots * HD
    spill = max(HD * first_head[d] - own * d for d in range(n))
    head_of = lambda d: (own * d + HD - 1) // HD
    head_at = HD * head_of(me)
    head_shift = head_at - own * me
    head_rows = HD * head_of(me + 1) - head_at

    x_own = tokens.reshape(part, width)
    x_near, x_far = gather_halves(x_own)
    runs = [
        [
            (c * width + HD * first_head[d], c * width + HD * first_head[d + 1], c * third)
            for c in range(3)
        ]
        for d in range(n)
    ]
    pieces = pack(w_qkv, me, True, runs, n, 3 * third)
    qkv_w = unpack(swap_packed(pieces)).reshape(width, 3 * third)

    vectors = (ln1_gain, ln1_bias, q_bias, v_bias, out_bias, ln2_gain, ln2_bias, proj_bias)
    lanes = 128 * -(-own // 128)
    packed = jnp.pad(jnp.stack(vectors), ((0, 0), (0, lanes - own)))
    packed = after(packed, pieces)
    packed_near, packed_far = gather_halves(packed[None])
    packed_all = jnp.concatenate([packed_near, packed_far], axis=0)
    everyone = jnp.stack([pick(packed_all, block_at(me, d, n)) for d in range(n)])
    gain_one, shift_one, bias_q, bias_v, bias_out, gain_two, shift_two, bias_proj = [
        everyone[:, i, :own].reshape(width).astype(F32) for i in range(len(vectors))
    ]
    live = jnp.arange(third) < head_rows
    own_heads = lambda v: jnp.where(
        live, lax.dynamic_slice_in_dim(jnp.pad(v, (0, third)), head_at, third, 0), 0.0
    )
    bias_heads = jnp.concatenate([own_heads(bias_q), jnp.zeros(third, F32), own_heads(bias_v)])

    def first_half(x):
        ln_b = layer_norm(x.astype(F32), gain_one, shift_one)[0].astype(BF16)
        return ln_b, (dot_nn(ln_b, qkv_w) + bias_heads).astype(BF16)

    ln_one_near, qkv_near = first_half(x_near)
    ln_one_far, qkv_far = first_half(x_far)
    qkv = jnp.concatenate([qkv_near, qkv_far], axis=0).reshape(n, part, 3 * third)

    fc_w = spread_columns(after(w_fc, x_near), own_hidden)
    g_own = grad_out.reshape(part, width)
    g_near, g_far = gather_halves(after(g_own, qkv_w))
    out_next = lax.ppermute(after(w_out, qkv_w)[:spill], "shard", [(i, i - 1) for i in range(1, n)])
    out_ext = jnp.concatenate([w_out, out_next, jnp.zeros((third, width), BF16)], axis=0)
    out_w = jnp.where(
        live[:, None], lax.dynamic_slice_in_dim(out_ext, head_shift, third, 0), 0.0
    ).astype(BF16)

    seg_row = segment_ids.reshape(1, length)
    seg_col = segment_ids.reshape(length, 1)
    me_word = me.astype(jnp.int32).reshape(1)
    attend, attend_back = attention_calls(n, part, slots, scale)
    attended, lse = attend(me_word, seg_row, seg_col, qkv)
    attended = attended.reshape(length, third)
    half = length // 2
    attn_own = finish_sums(
        chip_sums(dot_nn(attended[half:], out_w).astype(BF16), dot_nn(attended[:half], out_w))
    )
    resid_in = x_own.astype(F32)
    mid = resid_in + attn_own + bias_out

    ln_two, normed_two, inverse_two = layer_norm(mid, gain_two, shift_two)
    ln_two_near, ln_two_far = gather_halves(ln_two.astype(BF16))
    bias_fc = fc_bias.astype(F32)

    def middle(ln_b, g):
        pre = dot_nn(ln_b, fc_w) + bias_fc
        value, slope = gelu_both(pre)
        grad_pre = dot_nt(g, w_proj) * slope
        return value.astype(BF16), grad_pre.astype(BF16), jnp.sum(grad_pre, axis=0)

    hidden_near, grad_pre_near, sum_near = middle(ln_two_near, g_near)
    hidden_far, grad_pre_far, sum_far = middle(ln_two_far, g_far)
    grad_partial_far = dot_nt(grad_pre_far, fc_w).astype(BF16)
    two_total = chip_sums(grad_partial_far, dot_nt(grad_pre_near, fc_w))
    grad_ln_two = finish_sums(two_total)
    late = two_total
    part_proj = dot_tn(after(hidden_near, late), g_near)
    part_proj = (part_proj + dot_tn(after(hidden_far, late), g_far)).astype(BF16)
    part_proj = part_proj.reshape(own_hidden, n_rep, width // n_rep).transpose(1, 0, 2)
    total_proj = rep_scatter(part_proj)
    part_fc = dot_tn(after(ln_two_near, late), grad_pre_near)
    part_fc = (part_fc + dot_tn(after(ln_two_far, late), grad_pre_far)).astype(BF16)

    grad_mid = g_own.astype(F32) + norm_back(grad_ln_two, normed_two, inverse_two, gain_two)

    gm_near, gm_far = gather_halves(grad_mid.astype(BF16))
    out_far = dot_nn(after(hidden_far, late), w_proj).astype(BF16)
    out_near = dot_nn(after(hidden_near, late), w_proj)
    out_total = chip_sums(out_far, out_near)
    grad_att = jnp.concatenate(
        [dot_nt(gm_near, out_w).astype(BF16), dot_nt(gm_far, out_w).astype(BF16)], axis=0
    ).reshape(n, part, third)
    grad_qkv, head_sums = attend_back(me_word, seg_row, seg_col, qkv, grad_att, lse)
    grad_qkv = grad_qkv.reshape(length, 3 * third)
    grad_w = dot_tn(ln_one_near, grad_qkv[:half]) + dot_tn(ln_one_far, grad_qkv[half:])
    part_qkv = grad_w.astype(BF16)

    def spread(v):
        room = jnp.zeros(width + third, F32)
        return lax.dynamic_update_slice_in_dim(room, jnp.where(live, v, 0.0), head_at, 0)[:width]

    w_wide = qkv_w.astype(F32)
    shift_sum = jnp.sum(w_wide * head_sums[0], axis=1)
    gain_sum = (jnp.sum(w_wide * grad_w, axis=1) - shift_one * shift_sum) / gain_one
    grad_top = g_own.astype(F32)
    sums = [
        gain_sum,
        shift_sum,
        spread(head_sums[0, :third]),
        spread(head_sums[0, 2 * third :]),
        jnp.sum(grad_mid, axis=0),
        jnp.sum(grad_ln_two * normed_two, axis=0),
        jnp.sum(grad_ln_two, axis=0),
        jnp.sum(grad_top, axis=0),
    ]
    ratio = own_hidden // own
    room = 16 * -(-(len(sums) + ratio) // 16)
    columns = jnp.pad(jnp.stack(sums), ((0, 128 - len(sums)), (0, 0))).astype(BF16).T
    hidden_sum = (sum_near + sum_far).reshape(own, ratio)
    local_extra = jnp.pad(hidden_sum, ((0, 0), (len(sums), 128 - len(sums) - ratio)))
    outgoing = jnp.concatenate([part_qkv, columns], axis=1).reshape(n, own, -1)
    incoming = swap_packed(to_halves(outgoing))
    one_far = dot_nt(after(grad_qkv, outgoing)[half:], qkv_w).astype(BF16)
    one_near = dot_nt(after(grad_qkv, outgoing)[:half], qkv_w)
    attended_late = after(attended, outgoing)
    part_out = dot_tn(attended_late[:half], gm_near)
    part_out = (part_out + dot_tn(attended_late[half:], gm_far)).astype(BF16)
    shifted = lax.dynamic_update_slice_in_dim(
        jnp.zeros((own + spill + third, width), BF16), part_out, head_shift, 0
    )
    before = lax.ppermute(shifted[own : own + spill], "shard", [(i, i + 1) for i in range(n - 1)])
    own_out = shifted[:own] + jnp.pad(before, ((0, own - spill), (0, 0)))
    share = 3 * width // n_rep
    plan = []
    for q in range(n_rep):
        cols = []
        for c in range(3):
            for d in range(n):
                start = c * width + HD * first_head[d]
                lo = max(start, q * share)
                hi = min(start + HD * n_heads[d], (q + 1) * share)
                if lo < hi:
                    base = c * third - start
                    cols.append((d, base + lo, base + hi, lo - q * share))
        plan.append(cols)
    shares = to_shares(
        incoming, me_word, local_extra, own_out, plan, 3 * third, share, room
    )
    total = rep_scatter(shares)
    total_qkv = total[:, :share]
    smalls = total[:, share : share + room].T
    total_out = total[:, share + room :]
    total_fc = collect_rows(part_fc, own, hidden_width, total)
    grad_ln_one = finish_sums(chip_sums(one_far, one_near), shares)
    result = mid + bias_proj + finish_sums(out_total, shares)

    _, normed_one, inverse_one = layer_norm(resid_in, gain_one, shift_one)
    grad_in = grad_mid + norm_back(grad_ln_one, normed_one, inverse_one, gain_one)

    mine = [smalls[i] for i in range(len(sums))]
    mine_fc = total[:, share + len(sums) : share + len(sums) + ratio].reshape(own_hidden)
    return (
        result.reshape(seq_count, part, width),
        grad_in.reshape(seq_count, part, width),
        mine[0],
        mine[1],
        total_qkv,
        mine[2],
        mine[3],
        total_out,
        mine[4],
        mine[5],
        mine[6],
        total_fc,
        mine_fc,
        total_proj,
        mine[7],
    )


def solution(mesh):
    return jax.shard_map(
        local,
        mesh=mesh,
        in_specs=(
            P("rep", "shard", None),
            P("rep", None),
            P("shard"),
            P("shard"),
            P("shard", None),
            P("shard"),
            P("shard"),
            P("shard", None),
            P("shard"),
            P("shard"),
            P("shard"),
            P("shard", None),
            P("shard"),
            P("shard", None),
            P("shard"),
            P("rep", "shard", None),
        ),
        out_specs=(
            P("rep", "shard", None),
            P("rep", "shard", None),
            P("shard"),
            P("shard"),
            P("shard", "rep"),
            P("shard"),
            P("shard"),
            P("shard", "rep"),
            P("shard"),
            P("shard"),
            P("shard"),
            P("shard", "rep"),
            P("shard"),
            P("shard", "rep"),
            P("shard"),
        ),
        check_vma=False,
    )
```

profile of v0, /device:TPU:3, one launch (start us, length us, event | category | flops | bytes accessed | tf_op | source)
XLA Modules:
  0.0 585.3 jit_solution(2424844554499925075)
XLA Ops:
  51.1 11.5 %collective-permute-done.10.refs_4_ = bf16[2,200,768]{2,1,0:T(8,128)(2,1)} collective-permute-done((bf16[2,200,768]{2,1,0:T(8,128)(2,1)S(1)}, bf16[2,200,768]{2,1,0:T(8,128)(2,1)}, u32[]{:S(2)}, u32[]{:S(2)}) %collective-permute-start.10) | collective-permute-done | bytes 614432 | tf_op jit(solution)/shard_map/ppermute | solution.py:281
  62.6 12.5 %collective-permute-done.8.refs_2_ = bf16[2,200,768]{2,1,0:T(8,128)(2,1)} collective-permute-done((bf16[2,200,768]{2,1,0:T(8,128)(2,1)S(1)}, bf16[2,200,768]{2,1,0:T(8,128)(2,1)}, u32[]{:S(2)}, u32[]{:S(2)}) %collective-permute-start.8) | collective-permute-done | bytes 614432 | tf_op jit(solution)/shard_map/ppermute | solution.py:281
  99.1 23.0 %shard_map.273 = (bf16[8,128,256]{2,1,0:T(8,128)(2,1)}, f32[8,128,256]{2,1,0:T(8,128)}) custom-call(s32[1]{0:T(128)} %bitcast.1.base_ref.me_ref, s32[1,1024]{1,0:T(1,128)} %seg_row.3, s32[1024,1]{1,0:T(8,128)} %copy.76.seg_col, bf16[8,128,768]{2,1,0:T(8,128)(2,1)} %bitcast.129), custom_call_target="tpu_custom_call" | custom-call | flops 1073741824 | bytes 3670016 | tf_op jit(solution)/shard_map/pallas_call | solution.py:511
  147.3 7.8 %collective-permute-done.14 = bf16[128,1600]{0,1:T(8,128)(2,1)S(1)} collective-permute-done((bf16[128,1600]{0,1:T(8,128)(2,1)}, bf16[128,1600]{0,1:T(8,128)(2,1)S(1)}, u32[]{:S(2)}, u32[]{:S(2)}) %collective-permute-start.14) | collective-permute-done | bytes 409632 | tf_op jit(solution)/shard_map/ppermute | solution.py:281
  155.1 9.4 %collective-permute-done.16 = bf16[128,1600]{0,1:T(8,128)(2,1)} collective-permute-done((bf16[128,1600]{0,1:T(8,128)(2,1)}, bf16[128,1600]{0,1:T(8,128)(2,1)}, u32[]{:S(2)}, u32[]{:S(2)}) %collective-permute-start.16) | collective-permute-done | bytes 409632 | tf_op jit(solution)/shard_map/ppermute | solution.py:281
  172.2 5.7 collective-permute-done.17
  178.6 8.2 %collective-permute-done.19 = bf16[128,1600]{0,1:T(8,128)(2,1)S(1)} collective-permute-done((bf16[128,1600]{0,1:T(8,128)(2,1)S(1)}, bf16[128,1600]{0,1:T(8,128)(2,1)S(1)}, u32[]{:S(2)}, u32[]{:S(2)}) %collective-permute-start.19) | collective-permute-done | bytes 409632 | tf_op jit(solution)/shard_map/ppermute | solution.py:281
  197.3 7.1 %collective-permute-done.24 = bf16[128,1600]{0,1:T(8,128)(2,1)S(1)} collective-permute-done((bf16[128,1600]{0,1:T(8,128)(2,1)S(1)}, bf16[128,1600]{0,1:T(8,128)(2,1)S(1)}, u32[]{:S(2)}, u32[]{:S(2)}) %collective-permute-start.24) | collective-permute-done | bytes 409632 | tf_op jit(solution)/shard_map/ppermute | solution.py:281
  240.0 8.4 %collective-permute-done.29 = bf16[128,1600]{0,1:T(8,128)(2,1)S(1)} collective-permute-done((bf16[128,1600]{0,1:T(8,128)(2,1)S(1)}, bf16[128,1600]{0,1:T(8,128)(2,1)S(1)}, u32[]{:S(2)}, u32[]{:S(2)}) %collective-permute-start.29) | collective-permute-done | bytes 409632 | tf_op jit(solution)/shard_map/ppermute | solution.py:281
  248.3 9.7 %collective-permute-done.31 = bf16[128,1600]{0,1:T(8,128)(2,1)S(1)} collective-permute-done((bf16[128,1600]{0,1:T(8,128)(2,1)S(1)}, bf16[128,1600]{0,1:T(8,128)(2,1)S(1)}, u32[]{:S(2)}, u32[]{:S(2)}) %collective-permute-start.31) | collective-permute-done | bytes 409632 | tf_op jit(solution)/shard_map/ppermute | solution.py:281
  263.7 7.5 %collective-permute-done.32 = bf16[128,1600]{0,1:T(8,128)(2,1)S(1)} collective-permute-done((bf16[128,1600]{0,1:T(8,128)(2,1)S(1)}, bf16[128,1600]{0,1:T(8,128)(2,1)S(1)}, u32[]{:S(2)}, u32[]{:S(2)}) %collective-permute-start.32) | collective-permute-done | bytes 409632 | tf_op jit(solution)/shard_map/ppermute | solution.py:281
  271.2 8.6 %collective-permute-done.34 = bf16[128,1600]{0,1:T(8,128)(2,1)S(1)} collective-permute-done((bf16[128,1600]{0,1:T(8,128)(2,1)S(1)}, bf16[128,1600]{0,1:T(8,128)(2,1)S(1)}, u32[]{:S(2)}, u32[]{:S(2)}) %collective-permute-start.34) | collective-permute-done | bytes 409632 | tf_op jit(solution)/shard_map/ppermute | solution.py:281
  305.2 13.9 %shard_map.275 = (bf16[8,128,768]{2,1,0:T(8,128)(2,1)}, f32[8,768]{1,0:T(8,128)}) custom-call(s32[1]{0:T(128)} %bitcast.1.base_ref.me_ref, s32[1,1024]{1,0:T(1,128)} %seg_row.3, s32[1024,1]{1,0:T(8,128)} %copy.76.seg_col, bf16[8,128,768]{2,1,0:T(8,128)(2,1)} %bitcast.130, bf16[8,128,256]{2,1,0:T(8,128)(2,1)} %bitcast.138, ...), custom_call_target="tpu_custom_call" | custom-call | flops 2684354560 | bytes 4718592 | tf_op jit(solution)/shard_map/pallas_call | solution.py:552
  323.0 5.7 fusion.61
  334.0 7.4 %fusion.75 = (bf16[1600,768]{1,0:T(8,128)(2,1)}, f32[1600]{0:T(1024)S(1)}) fusion(bf16[1600,768]{1,0:T(8,128)(2,1)} %bitcast.107, f32[1600,768]{1,0:T(8,128)} %fusion.61, bf16[512,768]{1,0:T(8,128)(2,1)} %bitcast.135, bf16[512,1600]{0,1:T(8,128)(2,1)} %collective-permute-done.11, f32[512]{0:T(512)} %copy-done.63, f32[512]{0:T(512)S(1)} %copy-done.52, ...), kind=kOutput, calls=%fused_computation.219 | convolution fusion | flops 1269348864 | bytes 12278528 | tf_op jit(solution)/shard_map/dot_general | solution.py:60
  371.9 21.4 %collective-permute-done.40 = bf16[56,1600]{1,0:T(8,128)(2,1)} collective-permute-done((bf16[56,1600]{1,0:T(8,128)(2,1)}, bf16[56,1600]{1,0:T(8,128)(2,1)}, u32[]{:S(2)}, u32[]{:S(2)}) %collective-permute-start.40) | collective-permute-done | bytes 179232 | tf_op jit(solution)/shard_map/ppermute | solution.py:590
  417.5 5.3 copy.80
  435.1 6.3 %collective-permute-done.45 = bf16[128,1600]{0,1:T(8,128)(2,1)S(1)} collective-permute-done((bf16[128,1600]{0,1:T(8,128)(2,1)S(1)}, bf16[128,1600]{0,1:T(8,128)(2,1)S(1)}, u32[]{:S(2)}, u32[]{:S(2)}) %collective-permute-start.45) | collective-permute-done | bytes 409632 | tf_op jit(solution)/shard_map/ppermute | solution.py:281
  442.6 7.5 %collective-permute-done.47 = bf16[128,1600]{0,1:T(8,128)(2,1)S(1)} collective-permute-done((bf16[128,1600]{0,1:T(8,128)(2,1)S(1)}, bf16[128,1600]{0,1:T(8,128)(2,1)S(1)}, u32[]{:S(2)}, u32[]{:S(2)}) %collective-permute-start.47) | collective-permute-done | bytes 409632 | tf_op jit(solution)/shard_map/ppermute | solution.py:281
  452.3 6.6 %collective-permute-done.41 = bf16[128,1600]{0,1:T(8,128)(2,1)S(1)} collective-permute-done((bf16[128,1600]{0,1:T(8,128)(2,1)S(1)}, bf16[128,1600]{0,1:T(8,128)(2,1)S(1)}, u32[]{:S(2)}, u32[]{:S(2)}) %collective-permute-start.41) | collective-permute-done | bytes 409632 | tf_op jit(solution)/shard_map/ppermute | solution.py:281
  459.0 8.6 %collective-permute-done.43 = bf16[128,1600]{0,1:T(8,128)(2,1)S(1)} collective-permute-done((bf16[128,1600]{0,1:T(8,128)(2,1)S(1)}, bf16[128,1600]{0,1:T(8,128)(2,1)S(1)}, u32[]{:S(2)}, u32[]{:S(2)}) %collective-permute-start.43) | collective-permute-done | bytes 409632 | tf_op jit(solution)/shard_map/ppermute | solution.py:281
  474.5 48.3 %reduce-scatter.6.cloned.1.call-done = bf16[1,2,200,800]{3,2,1,0:T(8,128)(2,1)} async-done(((bf16[4,2,200,800]{3,2,1,0:T(8,128)(2,1)}), bf16[1,2,200,800]{3,2,1,0:T(8,128)(2,1)}) %reduce-scatter.6.cloned.1.call-update) | async-done | bytes 640016 | tf_op jit(solution)/shard_map/reduce_scatter | solution.py:354
  533.1 34.7 %collective-permute-done.48 = bf16[200,800]{1,0:T(8,128)(2,1)S(1)} collective-permute-done((bf16[200,800]{1,0:T(8,128)(2,1)}, bf16[200,800]{1,0:T(8,128)(2,1)S(1)}, u32[]{:S(2)}, u32[]{:S(2)}) %collective-permute-start.48) | collective-permute-done | bytes 320032 | tf_op jit(solution)/shard_map/ppermute | solution.py:364
  567.7 8.5 %collective-permute-done.49 = bf16[200,800]{1,0:T(8,128)(2,1)} collective-permute-done((bf16[200,800]{1,0:T(8,128)(2,1)S(1)}, bf16[200,800]{1,0:T(8,128)(2,1)}, u32[]{:S(2)}, u32[]{:S(2)}) %collective-permute-start.49) | collective-permute-done | bytes 320032 | tf_op jit(solution)/shard_map/ppermute | solution.py:364
  (393 shorter events, 276.8 us)
Async XLA Ops:
  7.2 205.1 %all-gather.3.cloned.1.call-start = ((), (), s32[]{:S(2)}) async-start(), calls=%async_computation.5 | async-start | bytes 3584000 | tf_op jit(solution)/shard_map/all_gather | solution.py:385
  41.9 48.7 %collective-permute-start.11 = (bf16[512,1600]{0,1:T(8,128)(2,1)}, bf16[512,1600]{0,1:T(8,128)(2,1)}, u32[]{:S(2)}, u32[]{:S(2)}) collective-permute-start(bf16[512,1600]{0,1:T(8,128)(2,1)} %get-tuple-element.90), channel_id=1, source_target_pairs={{0,4},{4,0},{8,12},{12,8},{16,20},{20,16},{24,28},{28,24},{1,5},{5... | collective-permute-start | bytes 4915208 | tf_op jit(solution)/shard_map/ppermute | solution.py:281
  47.8 27.3 %collective-permute-start.8 = (bf16[2,200,768]{2,1,0:T(8,128)(2,1)S(1)}, bf16[2,200,768]{2,1,0:T(8,128)(2,1)}, u32[]{:S(2)}, u32[]{:S(2)}) collective-permute-start(bf16[2,200,768]{2,1,0:T(8,128)(2,1)S(1)} %pad_maximum_fusion.11), channel_id=1, source_target_pairs={{0,8},{4,12},{8,0},{12,4},{16,24},{20,28},{24,16},{28,20},{1,9},{5... | collective-permute-start | bytes 1843208 | tf_op jit(solution)/shard_map/ppermute | solution.py:281
  48.1 28.1 %collective-permute-start.9 = (bf16[2,200,768]{2,1,0:T(8,128)(2,1)S(1)}, bf16[2,200,768]{2,1,0:T(8,128)(2,1)}, u32[]{:S(2)}, u32[]{:S(2)}) collective-permute-start(bf16[2,200,768]{2,1,0:T(8,128)(2,1)S(1)} %pad_maximum_fusion.12), channel_id=1, source_target_pairs={{0,16},{4,20},{8,24},{12,28},{16,0},{20,4},{24,8},{28,12},{1,17},{... | collective-permute-start | bytes 1843208 | tf_op jit(solution)/shard_map/ppermute | solution.py:281
  138.9 330.0 %reduce-scatter.8.cloned.1.call-start = ((), (), s32[]{:S(2)}) async-start(), calls=%async_computation.4 | async-start | bytes 3584000 | tf_op jit(solution)/shard_map/reduce_scatter | solution.py:354
  145.6 18.9 %collective-permute-start.16 = (bf16[128,1600]{0,1:T(8,128)(2,1)}, bf16[128,1600]{0,1:T(8,128)(2,1)}, u32[]{:S(2)}, u32[]{:S(2)}) collective-permute-start(bf16[128,1600]{0,1:T(8,128)(2,1)} %get-tuple-element.119), channel_id=1, source_target_pairs={{0,24},{4,28},{8,16},{12,20},{16,8},{20,12},{24,0},{28,4},{1,25},{... | collective-permute-start | bytes 1228808 | tf_op jit(solution)/shard_map/ppermute | solution.py:281
  170.5 25.1 %collective-permute-start.22 = (bf16[128,1600]{0,1:T(8,128)(2,1)S(1)}, bf16[128,1600]{0,1:T(8,128)(2,1)S(1)}, u32[]{:S(2)}, u32[]{:S(2)}) collective-permute-start(bf16[128,1600]{0,1:T(8,128)(2,1)S(1)} %bitcast.118), channel_id=1, source_target_pairs={{0,8},{4,12},{8,0},{12,4},{16,24},{20,28},{24,16},{28,20},{1,9},{5... | collective-permute-start | bytes 1228808 | tf_op jit(solution)/shard_map/ppermute | solution.py:281
  171.3 25.1 %collective-permute-start.23 = (bf16[128,1600]{0,1:T(8,128)(2,1)S(1)}, bf16[128,1600]{0,1:T(8,128)(2,1)S(1)}, u32[]{:S(2)}, u32[]{:S(2)}) collective-permute-start(bf16[128,1600]{0,1:T(8,128)(2,1)S(1)} %bitcast.119), channel_id=1, source_target_pairs={{0,16},{4,20},{8,24},{12,28},{16,0},{20,4},{24,8},{28,12},{1,17},{... | collective-permute-start | bytes 1228808 | tf_op jit(solution)/shard_map/ppermute | solution.py:281
  178.0 26.3 %collective-permute-start.24 = (bf16[128,1600]{0,1:T(8,128)(2,1)S(1)}, bf16[128,1600]{0,1:T(8,128)(2,1)S(1)}, u32[]{:S(2)}, u32[]{:S(2)}) collective-permute-start(bf16[128,1600]{0,1:T(8,128)(2,1)S(1)} %bitcast.121), channel_id=1, source_target_pairs={{0,24},{4,28},{8,16},{12,20},{16,8},{20,12},{24,0},{28,4},{1,25},{... | collective-permute-start | bytes 1228808 | tf_op jit(solution)/shard_map/ppermute | solution.py:281
  188.1 29.9 %collective-permute-start.26 = (bf16[512,1600]{0,1:T(8,128)(2,1)}, bf16[512,1600]{0,1:T(8,128)(2,1)}, u32[]{:S(2)}, u32[]{:S(2)}) collective-permute-start(bf16[512,1600]{0,1:T(8,128)(2,1)} %pad_maximum_fusion.3), channel_id=1, source_target_pairs={{0,4},{4,0},{8,12},{12,8},{16,20},{20,16},{24,28},{28,24},{1,5},{5... | collective-permute-start | bytes 4915208 | tf_op jit(solution)/shard_map/ppermute | solution.py:281
  238.8 19.2 %collective-permute-start.31 = (bf16[128,1600]{0,1:T(8,128)(2,1)S(1)}, bf16[128,1600]{0,1:T(8,128)(2,1)S(1)}, u32[]{:S(2)}, u32[]{:S(2)}) collective-permute-start(bf16[128,1600]{0,1:T(8,128)(2,1)S(1)} %get-tuple-element.116), channel_id=1, source_target_pairs={{0,24},{4,28},{8,16},{12,20},{16,8},{20,12},{24,0},{28,4},{1,25},{... | collective-permute-start | bytes 1228808 | tf_op jit(solution)/shard_map/ppermute | solution.py:281
  281.2 21.0 %collective-permute-start.35 = (bf16[512,1600]{0,1:T(8,128)(2,1)}, bf16[512,1600]{0,1:T(8,128)(2,1)}, u32[]{:S(2)}, u32[]{:S(2)}) collective-permute-start(bf16[512,1600]{0,1:T(8,128)(2,1)} %pad_maximum_fusion.4), channel_id=1, source_target_pairs={{0,4},{4,0},{8,12},{12,8},{16,20},{20,16},{24,28},{28,24},{1,5},{5... | collective-permute-start | bytes 4915208 | tf_op jit(solution)/shard_map/ppermute | solution.py:281
  299.1 172.1 %reduce-scatter.10.cloned.1.call-start = ((), (), s32[]{:S(2)}) async-start(), calls=%async_computation.6 | async-start | bytes 3328000
  358.6 36.8 %collective-permute-start.39 = (bf16[2,200,896]{2,1,0:T(8,128)(2,1)}, bf16[2,200,896]{2,1,0:T(8,128)(2,1)}, u32[]{:S(2)}, u32[]{:S(2)}) collective-permute-start(bf16[2,200,896]{2,1,0:T(8,128)(2,1)} %pad_maximum_fusion.10), channel_id=1, source_target_pairs={{0,24},{4,28},{8,16},{12,20},{16,8},{20,12},{24,0},{28,4},{1,25},{... | collective-permute-start | bytes 2150408 | tf_op jit(solution)/shard_map/ppermute | solution.py:281
  360.7 34.7 %collective-permute-start.38 = (bf16[2,200,896]{2,1,0:T(8,128)(2,1)}, bf16[2,200,896]{2,1,0:T(8,128)(2,1)}, u32[]{:S(2)}, u32[]{:S(2)}) collective-permute-start(bf16[2,200,896]{2,1,0:T(8,128)(2,1)} %pad_maximum_fusion.9), channel_id=1, source_target_pairs={{0,16},{4,20},{8,24},{12,28},{16,0},{20,4},{24,8},{28,12},{1,17},{... | collective-permute-start | bytes 2150408 | tf_op jit(solution)/shard_map/ppermute | solution.py:281
  362.8 32.6 %collective-permute-start.37 = (bf16[2,200,896]{2,1,0:T(8,128)(2,1)}, bf16[2,200,896]{2,1,0:T(8,128)(2,1)}, u32[]{:S(2)}, u32[]{:S(2)}) collective-permute-start(bf16[2,200,896]{2,1,0:T(8,128)(2,1)} %pad_maximum_fusion.8), channel_id=1, source_target_pairs={{0,8},{4,12},{8,0},{12,4},{16,24},{20,28},{24,16},{28,20},{1,9},{5... | collective-permute-start | bytes 2150408 | tf_op jit(solution)/shard_map/ppermute | solution.py:281
  365.2 28.1 %collective-permute-start.40 = (bf16[56,1600]{1,0:T(8,128)(2,1)}, bf16[56,1600]{1,0:T(8,128)(2,1)}, u32[]{:S(2)}, u32[]{:S(2)}) collective-permute-start(bf16[56,1600]{1,0:T(8,128)(2,1)} %slice.356), channel_id=1, source_target_pairs={{0,4},{4,8},{8,12},{12,16},{16,20},{20,24},{24,28},{1,5},{5,9},{9,... | collective-permute-start | bytes 537608 | tf_op jit(solution)/shard_map/ppermute | solution.py:590
  400.0 122.8 %reduce-scatter.6.cloned.1.call-start = ((), (), s32[]{:S(2)}) async-start(), calls=%async_computation.3 | async-start | bytes 3584000 | tf_op jit(solution)/shard_map/reduce_scatter | solution.py:354
  404.6 18.9 %collective-permute-start.28 = (bf16[512,1600]{0,1:T(8,128)(2,1)}, bf16[512,1600]{0,1:T(8,128)(2,1)}, u32[]{:S(2)}, u32[]{:S(2)}) collective-permute-start(bf16[512,1600]{0,1:T(8,128)(2,1)} %convolution_convert_fusion.1), channel_id=1, source_target_pairs={{0,4},{4,0},{8,12},{12,8},{16,20},{20,16},{24,28},{28,24},{1,5},{5... | collective-permute-start | bytes 4915208 | tf_op jit(solution)/shard_map/ppermute | solution.py:281
  433.5 25.5 %collective-permute-start.41 = (bf16[128,1600]{0,1:T(8,128)(2,1)S(1)}, bf16[128,1600]{0,1:T(8,128)(2,1)S(1)}, u32[]{:S(2)}, u32[]{:S(2)}) collective-permute-start(bf16[128,1600]{0,1:T(8,128)(2,1)S(1)} %get-tuple-element.47), channel_id=1, source_target_pairs={{0,8},{4,12},{8,0},{12,4},{16,24},{20,28},{24,16},{28,20},{1,9},{5... | collective-permute-start | bytes 1228808 | tf_op jit(solution)/shard_map/ppermute | solution.py:281
  433.6 25.4 %collective-permute-start.42 = (bf16[128,1600]{0,1:T(8,128)(2,1)S(1)}, bf16[128,1600]{0,1:T(8,128)(2,1)S(1)}, u32[]{:S(2)}, u32[]{:S(2)}) collective-permute-start(bf16[128,1600]{0,1:T(8,128)(2,1)S(1)} %get-tuple-element.48), channel_id=1, source_target_pairs={{0,16},{4,20},{8,24},{12,28},{16,0},{20,4},{24,8},{28,12},{1,17},{... | collective-permute-start | bytes 1228808 | tf_op jit(solution)/shard_map/ppermute | solution.py:281
  441.3 26.3 %collective-permute-start.43 = (bf16[128,1600]{0,1:T(8,128)(2,1)S(1)}, bf16[128,1600]{0,1:T(8,128)(2,1)S(1)}, u32[]{:S(2)}, u32[]{:S(2)}) collective-permute-start(bf16[128,1600]{0,1:T(8,128)(2,1)S(1)} %get-tuple-element.49), channel_id=1, source_target_pairs={{0,24},{4,28},{8,16},{12,20},{16,8},{20,12},{24,0},{28,4},{1,25},{... | collective-permute-start | bytes 1228808 | tf_op jit(solution)/shard_map/ppermute | solution.py:281
  524.6 43.1 %collective-permute-start.48 = (bf16[200,800]{1,0:T(8,128)(2,1)}, bf16[200,800]{1,0:T(8,128)(2,1)S(1)}, u32[]{:S(2)}, u32[]{:S(2)}) collective-permute-start(bf16[200,800]{1,0:T(8,128)(2,1)} %get-tuple-element.133), channel_id=1, source_target_pairs={{0,0},{1,8},{2,16},{3,24},{4,4},{5,12},{6,20},{7,28},{8,1},{9,9},{... | collective-permute-start | bytes 960008 | tf_op jit(solution)/shard_map/ppermute | solution.py:364
  527.1 49.2 %collective-permute-start.49 = (bf16[200,800]{1,0:T(8,128)(2,1)S(1)}, bf16[200,800]{1,0:T(8,128)(2,1)}, u32[]{:S(2)}, u32[]{:S(2)}) collective-permute-start(bf16[200,800]{1,0:T(8,128)(2,1)S(1)} %get-tuple-element.134), channel_id=1, source_target_pairs={{0,4},{1,12},{2,20},{3,28},{4,0},{5,8},{6,16},{7,24},{8,5},{9,13},... | collective-permute-start | bytes 960008 | tf_op jit(solution)/shard_map/ppermute | solution.py:364
  (95 other events, 1022.0 us)
Sparse Core Ops, SparseCore 0:
  139.0 73.2 all-gather.2
  299.2 65.2 reduce-scatter.7
  400.1 64.2 reduce-scatter.9
  466.5 56.1 reduce-scatter.5
where the time goes:
time: 591 us; the launch traced here: 585 us
  waiting for transfers between devices  257 us (43%)
  matrix products  84.2 us (14%)
  local copies, waits for them, and re-layouts  65 us (11%)
  starting transfers between devices  64.4 us (11%)
  Pallas kernels  51.6 us (9%)
  other arithmetic  48 us (8%)
  between operations  15.1 us (3%)
    ppermute x44, waiting for transfers between devices, exchange(): return lax.ppermute(x, 'shard', [(i, i ^ k) for i in range(n)])  138 us
    reduce_scatter x2, waiting for transfers between devices, rep_scatter(): return lax.psum_scatter(blocks, 'rep', scatter_dimension=0).astype(F32)  48.3 us
    ppermute x44, starting transfers between devices, exchange(): return lax.ppermute(x, 'shard', [(i, i ^ k) for i in range(n)])  46.4 us
    ppermute x4, waiting for transfers between devices, jointly(): return lax.ppermute(x, ('shard', 'rep'), pairs)  44.8 us
    dot_general x8, matrix products, dot_tn(): lax.dot_general(a, b, (((0,), (0,)), ((), ())), preferred_element_type=F32)  32.7 us
    dot_general x8, matrix products, dot_nn(): lax.dot_general(a, b, (((1,), (0,)), ((), ())), preferred_element_type=F32)  28.3 us
    dot_general x8, matrix products, dot_nt(): lax.dot_general(a, b, (((1,), (1,)), ((), ())), preferred_element_type=F32)  23.2 us
    pallas_call x1, Pallas kernels, local(): attended, lse = attend(me_word, seg_row, seg_col, qkv)  23 us
  transfers between devices with their start and end apart: 54, of which 27 were waited for; matrix products, arithmetic and copies ran while one was open for 27% of the time, Pallas kernels for 4%

commit v1 on v0

--- a/solution.py
+++ b/solution.py
@@ -395,26 +395,41 @@
     return jnp.stack([pick(blocks, jnp.bitwise_xor(me, k)) for k in order])
 
 
-def collect_rows(part, own_rows, total_columns, hold=None):
+def swap_direct(blocks):
+    n = lax.axis_size("shard")
+    me = lax.axis_index("shard")
+    picked = [pick(blocks, jnp.bitwise_xor(me, k)) for k in range(n)]
+    return [picked[0]] + [exchange(picked[k], k) for k in range(1, n)]
+
+
+def place_singles_kernel(me_ref, *refs):
+    for k, source in enumerate(refs[:-1]):
+        refs[-1][jnp.bitwise_xor(me_ref[0], k)] = source[...]
+
+
+def place_singles(sources):
+    shape = (len(sources), *sources[0].shape)
+    vm = pl.BlockSpec(memory_space=pltpu.VMEM)
+    return pl.pallas_call(
+        place_singles_kernel,
+        out_shape=jax.ShapeDtypeStruct(shape, BF16),
+        in_specs=[pl.BlockSpec(memory_space=pltpu.SMEM), *[vm] * len(sources)],
+        out_specs=vm,
+        cost_estimate=pl.CostEstimate(
+            flops=0, bytes_accessed=4 * math.prod(shape), transcendentals=0
+        ),
+    )(lax.axis_index("shard").astype(jnp.int32).reshape(1), *sources)
+
+
+def collect_rows(part, own_rows, total_columns):
     n, n_rep = lax.axis_size("shard"), lax.axis_size("rep")
     own = part.shape[1]
-    if n == 2 * n_rep:
-        summed = rep_scatter(part.reshape(n_rep, 2, own_rows, own)).astype(BF16)
-        if hold is not None:
-            summed = after(summed, hold)
-        even = jnp.bitwise_and(lax.axis_index("shard"), 1) == 0
-        pair = []
-        for k in range(2):
-            sent = jnp.where(even, summed[k], summed[1 - k])
-            pair.append(jointly(sent, lambda i, j, k=k: (2 * j + ((i & 1) ^ k), i >> 1)))
-        return jnp.concatenate(by_parity(pair), axis=1).astype(F32)
-    swapped = unpack(swap_packed(to_halves(part.reshape(n, own_rows, own))))
+    sources = swap_direct(part.reshape(n, own_rows, own))
+    swapped = place_singles(sources)
     if n_rep <= n:
-        swapped = swapped.reshape(n_rep, n // n_rep, own_rows, own)
-        total = rep_scatter(swapped)
-        return total.transpose(1, 0, 2).reshape(own_rows, total_columns // n_rep)
+        return swapped.reshape(n_rep, n // n_rep, own_rows, own)
     swapped = swapped.reshape(n, own_rows, n_rep // n, total_columns // n_rep)
-    return rep_scatter(swapped.transpose(0, 2, 1, 3).reshape(n_rep, own_rows, -1))
+    return swapped.transpose(0, 2, 1, 3).reshape(n_rep, 1, own_rows, -1)
 
 
 def after(value, *others):
@@ -546,13 +561,16 @@
     out_far = dot_nn(after(hidden_far, late), w_proj).astype(BF16)
     out_near = dot_nn(after(hidden_near, late), w_proj)
     out_total = chip_sums(out_far, out_near)
+    shares_fc = collect_rows(after(part_fc, gm_near), own, hidden_width)
+    total_fc = rep_scatter(shares_fc)
+    total_fc = total_fc.transpose(1, 0, 2).reshape(own, hidden_width // n_rep)
     grad_att = jnp.concatenate(
         [dot_nt(gm_near, out_w).astype(BF16), dot_nt(gm_far, out_w).astype(BF16)], axis=0
     ).reshape(n, part, third)
     grad_qkv, head_sums = attend_back(me_word, seg_row, seg_col, qkv, grad_att, lse)
     grad_qkv = grad_qkv.reshape(length, 3 * third)
     grad_w = dot_tn(ln_one_near, grad_qkv[:half]) + dot_tn(ln_one_far, grad_qkv[half:])
-    part_qkv = grad_w.astype(BF16)
+    part_qkv = after(grad_w.astype(BF16), shares_fc)
 
     def spread(v):
         room = jnp.zeros(width + third, F32)
@@ -575,10 +593,10 @@
     ratio = own_hidden // own
     room = 16 * -(-(len(sums) + ratio) // 16)
     columns = jnp.pad(jnp.stack(sums), ((0, 128 - len(sums)), (0, 0))).astype(BF16).T
-    hidden_sum = (sum_near + sum_far).reshape(own, ratio)
-    local_extra = jnp.pad(hidden_sum, ((0, 0), (len(sums), 128 - len(sums) - ratio)))
     outgoing = jnp.concatenate([part_qkv, columns], axis=1).reshape(n, own, -1)
     incoming = swap_packed(to_halves(outgoing))
+    hidden_sum = after(sum_near + sum_far, outgoing).reshape(own, ratio)
+    local_extra = jnp.pad(hidden_sum, ((0, 0), (len(sums), 128 - len(sums) - ratio)))
     one_far = dot_nt(after(grad_qkv, outgoing)[half:], qkv_w).astype(BF16)
     one_near = dot_nt(after(grad_qkv, outgoing)[:half], qkv_w)
     attended_late = after(attended, outgoing)
@@ -609,7 +627,6 @@
     total_qkv = total[:, :share]
     smalls = total[:, share : share + room].T
     total_out = total[:, share + room :]
-    total_fc = collect_rows(part_fc, own, hidden_width, total)
     grad_ln_one = finish_sums(chip_sums(one_far, one_near), shares)
     result = mid + bias_proj + finish_sums(out_total, shares)
 

time: 591 us -> 545 us (0.922)
  the two profiles are of different devices: /device:TPU:3 before, /device:TPU:0 now
where the time goes in v1:
time: 545 us; the launch traced here: 537 us
  waiting for transfers between devices  208 us (38%)
  matrix products  83.1 us (15%)
  local copies, waits for them, and re-layouts  72 us (13%)
  starting transfers between devices  56 us (10%)
  Pallas kernels  55 us (10%)
  other arithmetic  47.4 us (9%)
  between operations  15.1 us (3%)
    ppermute x51, waiting for transfers between devices, exchange(): return lax.ppermute(x, 'shard', [(i, i ^ k) for i in range(n)])  194 us
    ppermute x51, starting transfers between devices, exchange(): return lax.ppermute(x, 'shard', [(i, i ^ k) for i in range(n)])  49.3 us
    dot_general x8, matrix products, dot_tn(): lax.dot_general(a, b, (((0,), (0,)), ((), ())), preferred_element_type=F32)  30.3 us
    dot_general x8, matrix products, dot_nt(): lax.dot_general(a, b, (((1,), (1,)), ((), ())), preferred_element_type=F32)  26.8 us
    dot_general x8, matrix products, dot_nn(): lax.dot_general(a, b, (((1,), (0,)), ((), ())), preferred_element_type=F32)  26 us
    pallas_call x1, Pallas kernels, local(): attended, lse = attend(me_word, seg_row, seg_col, qkv)  23 us
    pallas_call x1, Pallas kernels, local(): attend_back(me_word, seg_row, seg_col, qkv, grad_att, lse)  13.9 us
  transfers between devices with their start and end apart: 59, of which 26 were waited for; matrix products, arithmetic and copies ran while one was open for 28% of the time, Pallas kernels for 5%

profile of v1, /device:TPU:0, one launch (start us, length us, event | category | flops | bytes accessed | tf_op | source)
XLA Modules:
  0.0 537.1 jit_solution(5122830927210591246)
XLA Ops:
  34.4 7.7 %collective-permute-done.1 = bf16[128,1600]{0,1:T(8,128)(2,1)} collective-permute-done((bf16[128,1600]{0,1:T(8,128)(2,1)S(1)}, bf16[128,1600]{0,1:T(8,128)(2,1)}, u32[]{:S(2)}, u32[]{:S(2)}) %collective-permute-start.1) | collective-permute-done | bytes 409632 | tf_op jit(solution)/shard_map/ppermute | solution.py:281
  53.1 12.1 %collective-permute-done.10.refs_4_ = bf16[2,200,768]{2,1,0:T(8,128)(2,1)} collective-permute-done((bf16[2,200,768]{2,1,0:T(8,128)(2,1)S(1)}, bf16[2,200,768]{2,1,0:T(8,128)(2,1)}, u32[]{:S(2)}, u32[]{:S(2)}) %collective-permute-start.10) | collective-permute-done | bytes 614432 | tf_op jit(solution)/shard_map/ppermute | solution.py:281
  65.2 12.7 %collective-permute-done.8.refs_2_ = bf16[2,200,768]{2,1,0:T(8,128)(2,1)} collective-permute-done((bf16[2,200,768]{2,1,0:T(8,128)(2,1)S(1)}, bf16[2,200,768]{2,1,0:T(8,128)(2,1)}, u32[]{:S(2)}, u32[]{:S(2)}) %collective-permute-start.8) | collective-permute-done | bytes 614432 | tf_op jit(solution)/shard_map/ppermute | solution.py:281
  98.8 23.0 %shard_map.273 = (bf16[8,128,256]{2,1,0:T(8,128)(2,1)}, f32[8,128,256]{2,1,0:T(8,128)}) custom-call(s32[1]{0:T(128)} %bitcast.1.base_ref.me_ref, s32[1,1024]{1,0:T(1,128)} %seg_row.3, s32[1024,1]{1,0:T(8,128)} %copy.87.seg_col, bf16[8,128,768]{2,1,0:T(8,128)(2,1)} %bitcast.147), custom_call_target="tpu_custom_call" | custom-call | flops 1073741824 | bytes 3670016 | tf_op jit(solution)/shard_map/pallas_call | solution.py:526
  146.6 8.6 %collective-permute-done.14 = bf16[128,1600]{0,1:T(8,128)(2,1)S(1)} collective-permute-done((bf16[128,1600]{0,1:T(8,128)(2,1)}, bf16[128,1600]{0,1:T(8,128)(2,1)S(1)}, u32[]{:S(2)}, u32[]{:S(2)}) %collective-permute-start.14) | collective-permute-done | bytes 409632 | tf_op jit(solution)/shard_map/ppermute | solution.py:281
  155.1 9.8 %collective-permute-done.15 = bf16[128,1600]{0,1:T(8,128)(2,1)} collective-permute-done((bf16[128,1600]{0,1:T(8,128)(2,1)}, bf16[128,1600]{0,1:T(8,128)(2,1)}, u32[]{:S(2)}, u32[]{:S(2)}) %collective-permute-start.15) | collective-permute-done | bytes 409632 | tf_op jit(solution)/shard_map/ppermute | solution.py:281
  174.7 5.8 %collective-permute-done.17 = bf16[128,1600]{0,1:T(8,128)(2,1)S(1)} collective-permute-done((bf16[128,1600]{0,1:T(8,128)(2,1)S(1)}, bf16[128,1600]{0,1:T(8,128)(2,1)S(1)}, u32[]{:S(2)}, u32[]{:S(2)}) %collective-permute-start.17) | collective-permute-done | bytes 409632 | tf_op jit(solution)/shard_map/ppermute | solution.py:281
  182.2 8.0 %collective-permute-done.18 = bf16[128,1600]{0,1:T(8,128)(2,1)S(1)} collective-permute-done((bf16[128,1600]{0,1:T(8,128)(2,1)S(1)}, bf16[128,1600]{0,1:T(8,128)(2,1)S(1)}, u32[]{:S(2)}, u32[]{:S(2)}) %collective-permute-start.18) | collective-permute-done | bytes 409632 | tf_op jit(solution)/shard_map/ppermute | solution.py:281
  191.8 6.4 %collective-permute-done.22 = bf16[128,1600]{0,1:T(8,128)(2,1)S(1)} collective-permute-done((bf16[128,1600]{0,1:T(8,128)(2,1)S(1)}, bf16[128,1600]{0,1:T(8,128)(2,1)S(1)}, u32[]{:S(2)}, u32[]{:S(2)}) %collective-permute-start.22) | collective-permute-done | bytes 409632 | tf_op jit(solution)/shard_map/ppermute | solution.py:281
  199.0 6.9 %collective-permute-done.23 = bf16[128,1600]{0,1:T(8,128)(2,1)S(1)} collective-permute-done((bf16[128,1600]{0,1:T(8,128)(2,1)S(1)}, bf16[128,1600]{0,1:T(8,128)(2,1)S(1)}, u32[]{:S(2)}, u32[]{:S(2)}) %collective-permute-start.23) | collective-permute-done | bytes 409632 | tf_op jit(solution)/shard_map/ppermute | solution.py:281
  207.6 6.9 %all-gather.3.cloned.1.call-done = bf16[8,200,800]{2,1,0:T(8,128)(2,1)} async-done(((bf16[2,200,800]{2,1,0:T(8,128)(2,1)}), bf16[8,200,800]{2,1,0:T(8,128)(2,1)}) %all-gather.3.cloned.1.call-update) | async-done | bytes 2560016 | tf_op jit(solution)/shard_map/all_gather | solution.py:385
  258.6 8.8 %collective-permute-done.29 = bf16[128,1600]{0,1:T(8,128)(2,1)S(1)} collective-permute-done((bf16[128,1600]{0,1:T(8,128)(2,1)S(1)}, bf16[128,1600]{0,1:T(8,128)(2,1)S(1)}, u32[]{:S(2)}, u32[]{:S(2)}) %collective-permute-start.29) | collective-permute-done | bytes 409632 | tf_op jit(solution)/shard_map/ppermute | solution.py:281
  267.4 9.5 %collective-permute-done.30 = bf16[128,1600]{0,1:T(8,128)(2,1)S(1)} collective-permute-done((bf16[128,1600]{0,1:T(8,128)(2,1)S(1)}, bf16[128,1600]{0,1:T(8,128)(2,1)S(1)}, u32[]{:S(2)}, u32[]{:S(2)}) %collective-permute-start.30) | collective-permute-done | bytes 409632 | tf_op jit(solution)/shard_map/ppermute | solution.py:281
  284.7 9.2 %collective-permute-done.32 = bf16[128,1600]{0,1:T(8,128)(2,1)} collective-permute-done((bf16[128,1600]{0,1:T(8,128)(2,1)}, bf16[128,1600]{0,1:T(8,128)(2,1)}, u32[]{:S(2)}, u32[]{:S(2)}) %collective-permute-start.32) | collective-permute-done | bytes 409632 | tf_op jit(solution)/shard_map/ppermute | solution.py:281
  293.9 8.5 %collective-permute-done.33 = bf16[128,1600]{0,1:T(8,128)(2,1)} collective-permute-done((bf16[128,1600]{0,1:T(8,128)(2,1)}, bf16[128,1600]{0,1:T(8,128)(2,1)}, u32[]{:S(2)}, u32[]{:S(2)}) %collective-permute-start.33) | collective-permute-done | bytes 409632 | tf_op jit(solution)/shard_map/ppermute | solution.py:281
  345.5 14.6 %collective-permute-done.40.refs_5_ = bf16[200,800]{1,0:T(8,128)(2,1)} collective-permute-done((bf16[200,800]{1,0:T(8,128)(2,1)}, bf16[200,800]{1,0:T(8,128)(2,1)}, u32[]{:S(2)}, u32[]{:S(2)}) %collective-permute-start.40) | collective-permute-done | bytes 320032 | tf_op jit(solution)/shard_map/ppermute | solution.py:281
  367.2 13.9 %shard_map.275 = (bf16[8,128,768]{2,1,0:T(8,128)(2,1)}, f32[8,768]{1,0:T(8,128)}) custom-call(s32[1]{0:T(128)} %bitcast.1.base_ref.me_ref, s32[1,1024]{1,0:T(1,128)} %seg_row.3, s32[1024,1]{1,0:T(8,128)} %copy.87.seg_col, bf16[8,128,768]{2,1,0:T(8,128)(2,1)} %bitcast.148, bf16[8,128,256]{2,1,0:T(8,128)(2,1)} %bitcast.155, ...), custom_call_target="tpu_custom_call" | custom-call | flops 2684354560 | bytes 4718592 | tf_op jit(solution)/shard_map/pallas_call | solution.py:570
  386.2 5.7 %fusion.75 = (bf16[1600,768]{1,0:T(8,128)(2,1)}, f32[1600]{0:T(1024)}) fusion(bf16[1600,768]{1,0:T(8,128)(2,1)S(1)} %bitcast.125, f32[1600,768]{1,0:T(8,128)S(1)} %fusion.61, bf16[512,768]{1,0:T(8,128)(2,1)S(1)} %bitcast.153, bf16[512,1600]{0,1:T(8,128)(2,1)} %collective-permute-done.11, f32[512]{0:T(512)S(1)} %copy-done.55, f32[512]{0:T(512)S(1)} %copy-done.43, ...), kind=kOutput, calls=%fused_computation.223 | convolution fusion | flops 1269348864 | bytes 12278528 | tf_op jit(solution)/shard_map/dot_general | solution.py:60
  436.3 7.7 %collective-permute-done.46.refs_4_ = bf16[2,200,896]{2,1,0:T(8,128)(2,1)} collective-permute-done((bf16[2,200,896]{2,1,0:T(8,128)(2,1)}, bf16[2,200,896]{2,1,0:T(8,128)(2,1)}, u32[]{:S(2)}, u32[]{:S(2)}) %collective-permute-start.46) | collective-permute-done | bytes 716832 | tf_op jit(solution)/shard_map/ppermute | solution.py:281
  444.0 14.3 %collective-permute-done.45.refs_3_ = bf16[2,200,896]{2,1,0:T(8,128)(2,1)} collective-permute-done((bf16[2,200,896]{2,1,0:T(8,128)(2,1)}, bf16[2,200,896]{2,1,0:T(8,128)(2,1)}, u32[]{:S(2)}, u32[]{:S(2)}) %collective-permute-start.45) | collective-permute-done | bytes 716832 | tf_op jit(solution)/shard_map/ppermute | solution.py:281
  475.8 7.4 %collective-permute-done.52 = bf16[128,1600]{0,1:T(8,128)(2,1)S(1)} collective-permute-done((bf16[128,1600]{0,1:T(8,128)(2,1)S(1)}, bf16[128,1600]{0,1:T(8,128)(2,1)S(1)}, u32[]{:S(2)}, u32[]{:S(2)}) %collective-permute-start.52) | collective-permute-done | bytes 409632 | tf_op jit(solution)/shard_map/ppermute | solution.py:281
  483.8 9.1 %collective-permute-done.53 = bf16[128,1600]{0,1:T(8,128)(2,1)S(1)} collective-permute-done((bf16[128,1600]{0,1:T(8,128)(2,1)S(1)}, bf16[128,1600]{0,1:T(8,128)(2,1)S(1)}, u32[]{:S(2)}, u32[]{:S(2)}) %collective-permute-start.53) | collective-permute-done | bytes 409632 | tf_op jit(solution)/shard_map/ppermute | solution.py:281
  500.8 8.6 %collective-permute-done.49 = bf16[128,1600]{0,1:T(8,128)(2,1)S(1)} collective-permute-done((bf16[128,1600]{0,1:T(8,128)(2,1)S(1)}, bf16[128,1600]{0,1:T(8,128)(2,1)S(1)}, u32[]{:S(2)}, u32[]{:S(2)}) %collective-permute-start.49) | collective-permute-done | bytes 409632 | tf_op jit(solution)/shard_map/ppermute | solution.py:281
  519.0 6.1 %reduce-scatter.10.cloned.1.call-done = bf16[1,200,1616]{2,1,0:T(8,128)(2,1)} async-done(((bf16[4,200,1616]{2,1,0:T(8,128)(2,1)}), bf16[1,200,1616]{2,1,0:T(8,128)(2,1)}) %reduce-scatter.10.cloned.1.call-update) | async-done | bytes 646416
  (393 shorter events, 290.6 us)
Async XLA Ops:
  7.2 207.3 %all-gather.3.cloned.1.call-start = ((), (), s32[]{:S(2)}) async-start(), calls=%async_computation.5 | async-start | bytes 3584000 | tf_op jit(solution)/shard_map/all_gather | solution.py:385
  45.2 45.1 %collective-permute-start.11 = (bf16[512,1600]{0,1:T(8,128)(2,1)}, bf16[512,1600]{0,1:T(8,128)(2,1)}, u32[]{:S(2)}, u32[]{:S(2)}) collective-permute-start(bf16[512,1600]{0,1:T(8,128)(2,1)} %get-tuple-element.94), channel_id=1, source_target_pairs={{0,4},{4,0},{8,12},{12,8},{16,20},{20,16},{24,28},{28,24},{1,5},{5... | collective-permute-start | bytes 4915208 | tf_op jit(solution)/shard_map/ppermute | solution.py:281
  48.9 29.0 %collective-permute-start.8 = (bf16[2,200,768]{2,1,0:T(8,128)(2,1)S(1)}, bf16[2,200,768]{2,1,0:T(8,128)(2,1)}, u32[]{:S(2)}, u32[]{:S(2)}) collective-permute-start(bf16[2,200,768]{2,1,0:T(8,128)(2,1)S(1)} %pad_maximum_fusion.11), channel_id=1, source_target_pairs={{0,8},{4,12},{8,0},{12,4},{16,24},{20,28},{24,16},{28,20},{1,9},{5... | collective-permute-start | bytes 1843208 | tf_op jit(solution)/shard_map/ppermute | solution.py:281
  50.6 27.3 %collective-permute-start.9 = (bf16[2,200,768]{2,1,0:T(8,128)(2,1)S(1)}, bf16[2,200,768]{2,1,0:T(8,128)(2,1)}, u32[]{:S(2)}, u32[]{:S(2)}) collective-permute-start(bf16[2,200,768]{2,1,0:T(8,128)(2,1)S(1)} %pad_maximum_fusion.12), channel_id=1, source_target_pairs={{0,16},{4,20},{8,24},{12,28},{16,0},{20,4},{24,8},{28,12},{1,17},{... | collective-permute-start | bytes 1843208 | tf_op jit(solution)/shard_map/ppermute | solution.py:281
  137.2 373.4 %reduce-scatter.8.cloned.1.call-start = ((), (), s32[]{:S(2)}) async-start(), calls=%async_computation.4 | async-start | bytes 3584000 | tf_op jit(solution)/shard_map/reduce_scatter | solution.py:354
  169.1 21.1 %collective-permute-start.18 = (bf16[128,1600]{0,1:T(8,128)(2,1)S(1)}, bf16[128,1600]{0,1:T(8,128)(2,1)S(1)}, u32[]{:S(2)}, u32[]{:S(2)}) collective-permute-start(bf16[128,1600]{0,1:T(8,128)(2,1)S(1)} %add_convert_fusion.4), channel_id=1, source_target_pairs={{0,16},{4,20},{8,24},{12,28},{16,0},{20,4},{24,8},{28,12},{1,17},{... | collective-permute-start | bytes 1228808 | tf_op jit(solution)/shard_map/ppermute | solution.py:281
  171.7 26.5 %collective-permute-start.22 = (bf16[128,1600]{0,1:T(8,128)(2,1)S(1)}, bf16[128,1600]{0,1:T(8,128)(2,1)S(1)}, u32[]{:S(2)}, u32[]{:S(2)}) collective-permute-start(bf16[128,1600]{0,1:T(8,128)(2,1)S(1)} %bitcast.136), channel_id=1, source_target_pairs={{0,8},{4,12},{8,0},{12,4},{16,24},{20,28},{24,16},{28,20},{1,9},{5... | collective-permute-start | bytes 1228808 | tf_op jit(solution)/shard_map/ppermute | solution.py:281
  172.6 33.3 %collective-permute-start.23 = (bf16[128,1600]{0,1:T(8,128)(2,1)S(1)}, bf16[128,1600]{0,1:T(8,128)(2,1)S(1)}, u32[]{:S(2)}, u32[]{:S(2)}) collective-permute-start(bf16[128,1600]{0,1:T(8,128)(2,1)S(1)} %bitcast.137), channel_id=1, source_target_pairs={{0,16},{4,20},{8,24},{12,28},{16,0},{20,4},{24,8},{28,12},{1,17},{... | collective-permute-start | bytes 1228808 | tf_op jit(solution)/shard_map/ppermute | solution.py:281
  180.6 26.2 %collective-permute-start.24 = (bf16[128,1600]{0,1:T(8,128)(2,1)S(1)}, bf16[128,1600]{0,1:T(8,128)(2,1)S(1)}, u32[]{:S(2)}, u32[]{:S(2)}) collective-permute-start(bf16[128,1600]{0,1:T(8,128)(2,1)S(1)} %bitcast.139), channel_id=1, source_target_pairs={{0,24},{4,28},{8,16},{12,20},{16,8},{20,12},{24,0},{28,4},{1,25},{... | collective-permute-start | bytes 1228808 | tf_op jit(solution)/shard_map/ppermute | solution.py:281
  191.7 28.5 %collective-permute-start.26 = (bf16[512,1600]{0,1:T(8,128)(2,1)}, bf16[512,1600]{0,1:T(8,128)(2,1)}, u32[]{:S(2)}, u32[]{:S(2)}) collective-permute-start(bf16[512,1600]{0,1:T(8,128)(2,1)} %pad_maximum_fusion.3), channel_id=1, source_target_pairs={{0,4},{4,0},{8,12},{12,8},{16,20},{20,16},{24,28},{28,24},{1,5},{5... | collective-permute-start | bytes 4915208 | tf_op jit(solution)/shard_map/ppermute | solution.py:281
  253.6 259.3 %reduce-scatter.6.cloned.1.call-start = ((), (), s32[]{:S(2)}) async-start(), calls=%async_computation.3 | async-start | bytes 3584000 | tf_op jit(solution)/shard_map/reduce_scatter | solution.py:354
  305.1 58.8 %collective-permute-start.35 = (bf16[512,1600]{0,1:T(8,128)(2,1)}, bf16[512,1600]{0,1:T(8,128)(2,1)}, u32[]{:S(2)}, u32[]{:S(2)}) collective-permute-start(bf16[512,1600]{0,1:T(8,128)(2,1)} %pad_maximum_fusion.4), channel_id=1, source_target_pairs={{0,4},{4,0},{8,12},{12,8},{16,20},{20,16},{24,28},{28,24},{1,5},{5... | collective-permute-start | bytes 4915208 | tf_op jit(solution)/shard_map/ppermute | solution.py:281
  326.7 33.4 %collective-permute-start.40 = (bf16[200,800]{1,0:T(8,128)(2,1)}, bf16[200,800]{1,0:T(8,128)(2,1)}, u32[]{:S(2)}, u32[]{:S(2)}) collective-permute-start(bf16[200,800]{1,0:T(8,128)(2,1)} %get-tuple-element.107), channel_id=1, source_target_pairs={{0,20},{4,16},{8,28},{12,24},{16,4},{20,0},{24,12},{28,8},{1,21},{... | collective-permute-start | bytes 960008 | tf_op jit(solution)/shard_map/ppermute | solution.py:281
  333.6 26.6 %collective-permute-start.41 = (bf16[200,800]{1,0:T(8,128)(2,1)}, bf16[200,800]{1,0:T(8,128)(2,1)}, u32[]{:S(2)}, u32[]{:S(2)}) collective-permute-start(bf16[200,800]{1,0:T(8,128)(2,1)} %get-tuple-element.106), channel_id=1, source_target_pairs={{0,24},{4,28},{8,16},{12,20},{16,8},{20,12},{24,0},{28,4},{1,25},{... | collective-permute-start | bytes 960008 | tf_op jit(solution)/shard_map/ppermute | solution.py:281
  363.7 161.5 %reduce-scatter.10.cloned.1.call-start = ((), (), s32[]{:S(2)}) async-start(), calls=%async_computation.6 | async-start | bytes 3328000
  408.1 55.6 %collective-permute-start.28 = (bf16[512,1600]{0,1:T(8,128)(2,1)}, bf16[512,1600]{0,1:T(8,128)(2,1)}, u32[]{:S(2)}, u32[]{:S(2)}) collective-permute-start(bf16[512,1600]{0,1:T(8,128)(2,1)} %convolution_convert_fusion.1), channel_id=1, source_target_pairs={{0,4},{4,0},{8,12},{12,8},{16,20},{20,16},{24,28},{28,24},{1,5},{5... | collective-permute-start | bytes 4915208 | tf_op jit(solution)/shard_map/ppermute | solution.py:281
  425.7 32.7 %collective-permute-start.45 = (bf16[2,200,896]{2,1,0:T(8,128)(2,1)}, bf16[2,200,896]{2,1,0:T(8,128)(2,1)}, u32[]{:S(2)}, u32[]{:S(2)}) collective-permute-start(bf16[2,200,896]{2,1,0:T(8,128)(2,1)} %pad_maximum_fusion.9), channel_id=1, source_target_pairs={{0,16},{4,20},{8,24},{12,28},{16,0},{20,4},{24,8},{28,12},{1,17},{... | collective-permute-start | bytes 2150408 | tf_op jit(solution)/shard_map/ppermute | solution.py:281
  427.2 31.2 %collective-permute-start.44 = (bf16[2,200,896]{2,1,0:T(8,128)(2,1)}, bf16[2,200,896]{2,1,0:T(8,128)(2,1)}, u32[]{:S(2)}, u32[]{:S(2)}) collective-permute-start(bf16[2,200,896]{2,1,0:T(8,128)(2,1)} %pad_maximum_fusion.8), channel_id=1, source_target_pairs={{0,8},{4,12},{8,0},{12,4},{16,24},{20,28},{24,16},{28,20},{1,9},{5... | collective-permute-start | bytes 2150408 | tf_op jit(solution)/shard_map/ppermute | solution.py:281
  434.3 33.2 %collective-permute-start.51 = (bf16[512,1600]{0,1:T(8,128)(2,1)}, bf16[512,1600]{0,1:T(8,128)(2,1)}, u32[]{:S(2)}, u32[]{:S(2)}) collective-permute-start(bf16[512,1600]{0,1:T(8,128)(2,1)} %convolution_convert_fusion.3), channel_id=1, source_target_pairs={{0,4},{4,0},{8,12},{12,8},{16,20},{20,16},{24,28},{28,24},{1,5},{5... | collective-permute-start | bytes 4915208 | tf_op jit(solution)/shard_map/ppermute | solution.py:281
  471.8 21.1 %collective-permute-start.53 = (bf16[128,1600]{0,1:T(8,128)(2,1)S(1)}, bf16[128,1600]{0,1:T(8,128)(2,1)S(1)}, u32[]{:S(2)}, u32[]{:S(2)}) collective-permute-start(bf16[128,1600]{0,1:T(8,128)(2,1)S(1)} %get-tuple-element.59), channel_id=1, source_target_pairs={{0,16},{4,20},{8,24},{12,28},{16,0},{20,4},{24,8},{28,12},{1,17},{... | collective-permute-start | bytes 1228808 | tf_op jit(solution)/shard_map/ppermute | solution.py:281
  472.0 20.9 %collective-permute-start.54 = (bf16[128,1600]{0,1:T(8,128)(2,1)S(1)}, bf16[128,1600]{0,1:T(8,128)(2,1)S(1)}, u32[]{:S(2)}, u32[]{:S(2)}) collective-permute-start(bf16[128,1600]{0,1:T(8,128)(2,1)S(1)} %get-tuple-element.60), channel_id=1, source_target_pairs={{0,24},{4,28},{8,16},{12,20},{16,8},{20,12},{24,0},{28,4},{1,25},{... | collective-permute-start | bytes 1228808 | tf_op jit(solution)/shard_map/ppermute | solution.py:281
  474.5 26.2 %collective-permute-start.48 = (bf16[128,1600]{0,1:T(8,128)(2,1)S(1)}, bf16[128,1600]{0,1:T(8,128)(2,1)S(1)}, u32[]{:S(2)}, u32[]{:S(2)}) collective-permute-start(bf16[128,1600]{0,1:T(8,128)(2,1)S(1)} %get-tuple-element.54), channel_id=1, source_target_pairs={{0,8},{4,12},{8,0},{12,4},{16,24},{20,28},{24,16},{28,20},{1,9},{5... | collective-permute-start | bytes 1228808 | tf_op jit(solution)/shard_map/ppermute | solution.py:281
  475.6 33.8 %collective-permute-start.49 = (bf16[128,1600]{0,1:T(8,128)(2,1)S(1)}, bf16[128,1600]{0,1:T(8,128)(2,1)S(1)}, u32[]{:S(2)}, u32[]{:S(2)}) collective-permute-start(bf16[128,1600]{0,1:T(8,128)(2,1)S(1)} %get-tuple-element.55), channel_id=1, source_target_pairs={{0,16},{4,20},{8,24},{12,28},{16,0},{20,4},{24,8},{28,12},{1,17},{... | collective-permute-start | bytes 1228808 | tf_op jit(solution)/shard_map/ppermute | solution.py:281
  483.2 26.2 %collective-permute-start.50 = (bf16[128,1600]{0,1:T(8,128)(2,1)S(1)}, bf16[128,1600]{0,1:T(8,128)(2,1)S(1)}, u32[]{:S(2)}, u32[]{:S(2)}) collective-permute-start(bf16[128,1600]{0,1:T(8,128)(2,1)S(1)} %get-tuple-element.56), channel_id=1, source_target_pairs={{0,24},{4,28},{8,16},{12,20},{16,8},{20,12},{24,0},{28,4},{1,25},{... | collective-permute-start | bytes 1228808 | tf_op jit(solution)/shard_map/ppermute | solution.py:281
  (94 other events, 1166.2 us)
Sparse Core Ops, SparseCore 0:
  137.4 77.0 all-gather.2
  253.7 67.0 reduce-scatter.7
  363.8 65.3 reduce-scatter.5
  463.2 61.9 reduce-scatter.9
